TPU v7x, 32 devices: a whole 2x2x4 slice. The times are simulated.
32 devices in a mesh: groups: 2 (over y), replay: 4 (over z), module: 2 (over x), half: 2 (over core).
Axes of the slice: x: 2, y: 2, z: 4, core: 2. Of those that a mesh axis runs over, the one named last changes fastest.
Arguments:
- new_factors: bfloat16 [128, 2, 64, 128], P(('groups', 'replay', 'module')), parts along dimension 0, may hold values from -0.5 to 0.5
- new_counts: int32 [128], P(('groups', 'replay', 'module')), parts along dimension 0, may hold values from 32 to 64
- new_ids: int32 [128], P(('groups', 'module', 'half')), parts along dimension 0, may hold values from 0 to 3071
- replay_grads: bfloat16 [6144, 2, 4096], P(('groups', 'replay'), 'module', 'half'), parts along dimension 0, may hold values from -0.75 to 0.75
- replay_ids: int32 [6144], P(('groups', 'replay')), parts along dimension 0, may hold values from 0 to 3071
- slot_module: int32 [2], replicated, may hold values from 0 to 1, each once
- output_inverse: float32 [2, 64, 64], replicated, as said below
- input_inverse: float32 [2, 64, 64], replicated, as said below
Outputs:
- scores: float32 [128, 3072], P(('groups', 'module', 'half'), 'replay'), parts along dimension 0
There are 2 independent parts, one for each index of `groups`. A program takes and returns all parts, laid end to end along the dimension named above; an argument that names none is the same for every part. Nothing has to cross between parts.
Inputs may be any that keep to these rules, and one draw needn't show every extreme that they name: `new_counts`: each new example has at least half of its token slots live, the live ones first. `slot_module`: each module sits in exactly one slot. `output_inverse`: symmetric with a positive diagonal. `input_inverse`: symmetric with a positive diagonal.
All inputs are finite; a program needn't handle non-finite values.
Results may differ from a plain program's by a relative error of at most 0.0029.
Values may be sent and summed in bfloat16 or wider, within the bound.
A program may use at most 64 MiB of HBM per device.

v0:
```python
import functools

import jax
import jax.numpy as jnp
from jax import lax
from jax.experimental import pallas as pl
from jax.experimental.pallas import tpu as pltpu
from jax.sharding import PartitionSpec as P

MESH = pl.DeviceIdType.MESH
UNROLL = 16
EARLY = 1
LATE = 2


def each(count, step):
    if count <= UNROLL:
        for index in range(count):
            step(index)
    else:
        def one(index, carry):
            step(index)
            return carry

        lax.fori_loop(0, count, one, 0)


def parts_of(value):
    high = value.astype(jnp.bfloat16)
    low = (value - high.astype(jnp.float32)).astype(jnp.bfloat16)
    return high, low


def kernel(
    sizes,
    slot_module_hbm,
    counts_hbm,
    factors_hbm,
    replay_hbm,
    left_hbm,
    right_hbm,
    out_ref,
    slot_module,
    counts,
    factors,
    replay,
    left,
    right,
    rows_f32,
    outgoing,
    blocks,
    part,
    arrived,
    load_sem,
    send_sem,
    recv_sem,
    score_send_sem,
    score_recv_sem,
):
    replays, modules, halves, chunk = sizes
    z, x, h = lax.axis_index("replay"), lax.axis_index("module"), lax.axis_index("half")
    block = z * modules + x
    owner = x * halves + h
    owners = modules * halves
    examples, _, tokens, width = factors.shape
    feat = width // 2
    share = replay.shape[1] // feat
    columns = replay.shape[0]
    chunks = columns // chunk

    barrier = pltpu.get_barrier_semaphore()

    def greet_block(offset):
        target = lax.rem(block + offset + 1, replays * modules)
        pl.semaphore_signal(
            barrier,
            inc=1,
            device_id={"replay": target // modules, "module": lax.rem(target, modules)},
            device_id_type=MESH,
        )

    def greet_owner(offset):
        index = lax.rem(h + offset % (halves - 1) + 1, halves)
        pl.semaphore_signal(
            barrier,
            inc=1,
            device_id={"module": offset // (halves - 1), "half": index},
            device_id_type=MESH,
        )

    each(replays * modules - 1, greet_block)
    for offset in range(modules * (halves - 1)):
        greet_owner(offset)

    small_loads = [
        pltpu.make_async_copy(factors_hbm, factors, load_sem.at[0]),
        pltpu.make_async_copy(left_hbm, left, load_sem.at[1]),
        pltpu.make_async_copy(right_hbm, right, load_sem.at[2]),
        pltpu.make_async_copy(slot_module_hbm, slot_module, load_sem.at[4]),
        pltpu.make_async_copy(counts_hbm, counts, load_sem.at[5]),
    ]
    for load in small_loads:
        load.start()
    replay_load = pltpu.make_async_copy(replay_hbm, replay, load_sem.at[3])
    replay_load.start()

    for load in small_loads:
        load.wait()

    pair = 128 // tokens
    lane = lax.broadcasted_iota(jnp.int32, (share, 128), 1)
    zero = jnp.zeros((), jnp.bfloat16)
    low_lanes = lax.broadcasted_iota(jnp.int32, (examples, 2 * feat), 1) < feat

    def precondition(slot):
        module = slot_module[slot]
        entries = factors[:, module].reshape(examples * tokens, width)
        doubled = jnp.concatenate([entries, entries], axis=1)
        right_high, right_low = parts_of(right[module])
        blank = jnp.zeros((feat, feat), jnp.bfloat16)
        right_rows = jnp.concatenate([right_high, blank, right_low, blank], axis=0)
        right_rows = jnp.concatenate([right_rows, right_rows], axis=1)
        v = jnp.dot(doubled, right_rows, preferred_element_type=jnp.float32)
        left_high, left_low = parts_of(left[module, pl.ds(pl.multiple_of(h * share, share), share), :])
        left_blank = jnp.zeros((share, feat), jnp.bfloat16)
        left_columns = jnp.concatenate([left_blank, left_high, left_blank, left_low], axis=1)
        u = lax.dot_general(
            left_columns, doubled, (((1,), (1,)), ((), ())), preferred_element_type=jnp.float32
        )
        v_high, v_low = parts_of(v)
        for group in range(examples // pair):
            u_pair = u[:, group * 128 : (group + 1) * 128]
            masked = []
            for inner in range(pair):
                count = counts[group * pair + inner]
                first = inner * tokens
                keep = (lane >= first) & (lane < first + count)
                masked.append(jnp.where(keep, u_pair, 0.0))
            u_high, u_low = parts_of(jnp.concatenate(masked, axis=0))
            lhs = jnp.concatenate([u_high, u_high, u_low], axis=1)
            span = slice(group * 128, (group + 1) * 128)
            rhs = jnp.concatenate([v_high[span], v_low[span], v_high[span]], axis=0)
            rows_f32[pl.ds(group * pair * share, pair * share), :] = jnp.dot(
                lhs, rhs, preferred_element_type=jnp.float32
            )
        for q in range(share // 2):
            even = rows_f32[pl.ds(2 * q, examples, stride=share), :]
            odd = rows_f32[pl.ds(2 * q + 1, examples, stride=share), :]
            outgoing[slot, :, q * 2 * feat : (q + 1) * 2 * feat] = jnp.where(low_lanes, even, odd).astype(
                jnp.bfloat16
            )

    def block_copy(slot, target_z):
        target = target_z * modules + slot
        return pltpu.make_async_remote_copy(
            src_ref=outgoing.at[slot],
            dst_ref=blocks.at[block],
            send_sem=send_sem.at[target],
            recv_sem=recv_sem.at[block],
            device_id={"replay": target_z, "module": slot},
            device_id_type=MESH,
        )

    for slot in range(modules):
        precondition(slot)
    blocks[block] = outgoing[x]
    pl.semaphore_wait(barrier, replays * modules - 1 + modules * (halves - 1))

    def neighbour(step):
        if replays & (replays - 1):
            return lax.rem(z + step, replays)
        other, bit = z, 1
        while bit < replays:
            other = other + bit * ((step // bit) % 2) * (1 - 2 * ((z // bit) % 2))
            bit *= 2
        return other

    def send_blocks(step):
        for offset in range(1, modules):
            block_copy(lax.rem(x + offset, modules), neighbour(step)).start()
        if not (isinstance(step, int) and step == 0):
            block_copy(x, neighbour(step)).start()

    send_blocks(0)
    each(replays - 1, lambda index: send_blocks(1 + (index + 1) % (replays - 1)))

    per_owner = replays // owners
    step_rows = modules * examples

    def await_block(slot, source):
        pltpu.make_async_remote_copy(
            src_ref=outgoing.at[0],
            dst_ref=blocks.at[source],
            send_sem=send_sem.at[source],
            recv_sem=recv_sem.at[source],
            device_id={"replay": source // modules, "module": slot},
            device_id_type=MESH,
        ).wait_recv()

    def score_copy(source, c):
        cut = pl.ds(c * chunk, chunk)
        target = source // per_owner
        return pltpu.make_async_remote_copy(
            src_ref=part.at[pl.ds(pl.multiple_of(source * step_rows, step_rows), step_rows), cut],
            dst_ref=arrived.at[
                owner, pl.ds(pl.multiple_of((source % per_owner) * step_rows, step_rows), step_rows), cut
            ],
            send_sem=score_send_sem.at[source, c],
            recv_sem=score_recv_sem.at[owner, source % per_owner, c],
            device_id={"module": target // halves, "half": target % halves},
            device_id_type=MESH,
        )

    def score_await(source, inner, c):
        cut = pl.ds(c * chunk, chunk)
        return pltpu.make_async_remote_copy(
            src_ref=part.at[pl.ds(0, step_rows), cut],
            dst_ref=arrived.at[source, pl.ds(inner * step_rows, step_rows), cut],
            send_sem=score_send_sem.at[0, c],
            recv_sem=score_recv_sem.at[source, inner, c],
            device_id={"module": source // halves, "half": source % halves},
            device_id_type=MESH,
        )

    replay_load.wait()

    def await_step(step):
        source = neighbour(step)
        for offset in range(1, modules):
            slot = lax.rem(x + offset, modules)
            await_block(slot, source * modules + slot)
        if not (isinstance(step, int) and step == 0):
            await_block(x, source * modules + x)

    def score_steps(first, count, pieces):
        sources = [neighbour(first + inner) for inner in range(count)]
        lhs = jnp.concatenate(
            [blocks[source * modules + slot] for source in sources for slot in range(modules)], axis=0
        )
        for piece in range(pieces):
            span = columns // pieces
            cut = slice(piece * span, (piece + 1) * span)
            scores = lax.dot_general(
                lhs, replay[cut, :], (((1,), (1,)), ((), ())), preferred_element_type=jnp.float32
            )
            for inner, source in enumerate(sources):
                part[pl.ds(pl.multiple_of(source * step_rows, step_rows), step_rows), cut] = scores[
                    inner * step_rows : (inner + 1) * step_rows
                ]
            for source in sources:

                @pl.when(source // per_owner != owner)
                def _():
                    for c in range(piece * span // chunk, (piece + 1) * span // chunk):
                        score_copy(source, c).start()

    batch = 2 if replays % 2 == 0 else 1
    for inner in range(batch):
        await_step(inner)
    score_steps(0, batch, EARLY)

    def later(index):
        for inner in range(batch):
            await_step((index + 1) * batch + inner)
        score_steps((index + 1) * batch, batch, LATE)

    each(replays // batch - 1, later)

    for c in range(chunks):
        cut = slice(c * chunk, (c + 1) * chunk)
        for inner in range(per_owner):
            span = pl.ds(inner * step_rows, step_rows)
            first = owner * per_owner * step_rows + inner * step_rows
            summed = part[pl.ds(pl.multiple_of(first, step_rows), step_rows), cut]
            for offset in range(1, owners):
                source = lax.rem(owner + offset, owners)
                score_await(source, inner, c).wait_recv()
                summed = summed + arrived[source, span, cut]
            out_ref[span, cut] = summed

    def await_sent(step):
        source = neighbour(step)
        for offset in range(1, modules):
            block_copy(lax.rem(x + offset, modules), source).wait_send()
        if not (isinstance(step, int) and step == 0):
            block_copy(x, source).wait_send()

        @pl.when(source // per_owner != owner)
        def _():
            for c in range(chunks):
                score_copy(source, c).wait_send()

    await_sent(0)
    each(replays - 1, lambda index: await_sent(index + 1))


def pin(array):
    return pltpu.with_memory_space_constraint(array, pltpu.HBM)


def body(
    replays,
    modules,
    halves,
    new_factors,
    new_counts,
    new_ids,
    replay_grads,
    replay_ids,
    slot_module,
    output_inverse,
    input_inverse,
):
    examples, _, _, width = new_factors.shape
    feat = width // 2
    columns, _, depth = replay_grads.shape
    share = depth // feat
    total = replays * modules * examples
    owners = modules * halves
    rows = total // owners
    chunk = 384 if columns % 384 == 0 else columns // LATE
    hbm = pl.BlockSpec(memory_space=pltpu.HBM)
    summed = pl.pallas_call(
        functools.partial(kernel, (replays, modules, halves, chunk)),
        out_shape=jax.ShapeDtypeStruct((rows, columns), jnp.float32),
        in_specs=[hbm] * 6,
        out_specs=pl.BlockSpec(memory_space=pltpu.VMEM),
        scratch_shapes=[
            pltpu.SMEM(slot_module.shape, jnp.int32),
            pltpu.SMEM(new_counts.shape, jnp.int32),
            pltpu.VMEM(new_factors.shape, jnp.bfloat16),
            pltpu.VMEM((columns, depth), jnp.bfloat16),
            pltpu.VMEM(output_inverse.shape, jnp.float32),
            pltpu.VMEM(input_inverse.shape, jnp.float32),
            pltpu.VMEM((examples * share, 2 * feat), jnp.float32),
            pltpu.VMEM((modules, examples, depth), jnp.bfloat16),
            pltpu.VMEM((replays * modules, examples, depth), jnp.bfloat16),
            pltpu.VMEM((total, columns), jnp.float32),
            pltpu.VMEM((owners, rows, columns), jnp.float32),
            pltpu.SemaphoreType.DMA((6,)),
            pltpu.SemaphoreType.DMA((replays * modules,)),
            pltpu.SemaphoreType.DMA((replays * modules,)),
            pltpu.SemaphoreType.DMA((replays, columns // chunk)),
            pltpu.SemaphoreType.DMA((owners, replays // owners, columns // chunk)),
        ],
        compiler_params=pltpu.CompilerParams(
            collective_id=0, has_side_effects=True, vmem_limit_bytes=24 * 1024 * 1024
        ),
        name="attribution",
    )(
        pin(slot_module),
        pin(new_counts),
        pin(new_factors),
        pin(replay_grads.reshape(columns, depth)),
        pin(output_inverse),
        pin(input_inverse),
    )
    self_pairs = new_ids[:, None] == replay_ids[None, :]
    return jnp.where(self_pairs, jnp.zeros((), jnp.float32), summed)


def solution(mesh):
    in_specs = (
        P(("groups", "replay", "module"), None, None, None),
        P(("groups", "replay", "module")),
        P(("groups", "module", "half")),
        P(("groups", "replay"), "module", "half"),
        P(("groups", "replay")),
        P(),
        P(),
        P(),
    )
    out_specs = P(("groups", "module", "half"), "replay")
    return jax.shard_map(
        functools.partial(body, mesh.shape["replay"], mesh.shape["module"], mesh.shape["half"]),
        mesh=mesh,
        in_specs=in_specs,
        out_specs=out_specs,
        check_vma=False,
    )
```

profile of v0, /device:TPU:0, one launch (start us, length us, event | category | flops | bytes accessed | tf_op | source)
XLA Modules:
  0.0 16.1 jit_solution(11520799467655670912)
XLA Ops:
  0.0 0.0 copy-start
  0.0 0.0 copy-start.1
  0.0 15.4 %attribution.1 = f32[16,768]{1,0:T(8,128)S(1)} custom-call(s32[2]{0:T(128)} %slot_module_hbm.1, s32[8]{0:T(128)} %counts_hbm.1, bf16[8,2,64,128]{3,2,1,0:T(8,128)(2,1)} %factors_hbm.1, bf16[768,2048]{1,0:T(8,128)(2,1)} %bitcast.1, f32[2,64,64]{2,1,0:T(8,128)} %left_hbm.1, f32[2,64,64]{2,1,0:T(8,128)} %right_hbm.1), custom_call_target="tpu_custom_call" | custom-call | tf_op jit(solution)/shard_map/attribution/pallas_call | solution.py:323
  15.4 0.0 copy-done
  15.4 0.0 copy-done.1
  15.4 0.7 %compare_select_fusion = f32[16,768]{1,0:T(8,128)} fusion(f32[16,768]{1,0:T(8,128)S(1)} %attribution.1, s32[768]{0:T(1024)S(1)} %copy-done, s32[16]{0:T(128)S(1)} %copy-done.1), kind=kLoop, calls=%fused_computation | loop fusion | flops 24576 | bytes 101440 | tf_op jit(solution)/shard_map/jit(_where)/select_n | solution.py:359
Async XLA Ops:
  0.0 15.4 %copy-start = (s32[768]{0:T(1024)S(1)}, s32[768]{0:T(1024)}, u32[]{:S(2)}) copy-start(s32[768]{0:T(1024)} %param.12) | copy-start | bytes 9220
  0.0 15.4 %copy-start.1 = (s32[16]{0:T(128)S(1)}, s32[16]{0:T(128)}, u32[]{:S(2)}) copy-start(s32[16]{0:T(128)} %param.10) | copy-start | bytes 196
where the time goes:
time: 16.3 us; the launch traced here: 16.1 us
  Pallas kernels  15.4 us (94%)
  other arithmetic  0.69 us (4%)
    pallas_call x1, Pallas kernels, body(): pl.pallas_call(functools.partial(kernel, (replays, modules, halves, chunk...  15.4 us
    select_n x1, other arithmetic, body(): return jnp.where(self_pairs, jnp.zeros((), jnp.float32), summed)  0.69 us

commit v1 on v0

v1 whole, which is shorter than its diff:
```python
import functools

import jax
import jax.numpy as jnp
from jax import lax
from jax.experimental import pallas as pl
from jax.experimental.pallas import tpu as pltpu
from jax.sharding import PartitionSpec as P

MESH = pl.DeviceIdType.MESH
UNROLL = 16
PIECES = 2
TERM = jnp.bfloat16


def each(count, step):
    if count <= UNROLL:
        for index in range(count):
            step(index)
    else:
        def one(index, carry):
            step(index)
            return carry

        lax.fori_loop(0, count, one, 0)


def parts_of(value):
    high = value.astype(jnp.bfloat16)
    low = (value - high.astype(jnp.float32)).astype(jnp.bfloat16)
    return high, low


def kernel(
    sizes,
    slot_module_hbm,
    counts_hbm,
    factors_hbm,
    replay_hbm,
    left_hbm,
    right_hbm,
    out_ref,
    slot_module,
    counts,
    factors,
    replay,
    replay_t,
    inverses,
    rows_f32,
    outgoing,
    blocks,
    part,
    terms,
    arrived,
    load_sem,
    ready,
    send_sem,
    recv_sem,
    score_recv_sem,
):
    replays, modules, halves, chunk = sizes
    z, x, h = lax.axis_index("replay"), lax.axis_index("module"), lax.axis_index("half")
    block = z * modules + x
    owner = x * halves + h
    owners = modules * halves
    examples, _, tokens, width = factors.shape
    feat = width // 2
    share = replay.shape[1] // feat
    columns = replay.shape[0]
    chunks = columns // chunk
    last = replays - 1

    left, right = inverses.at[0], inverses.at[1]
    for source, target, index in (
        (factors_hbm, factors, 0),
        (left_hbm, left, 1),
        (right_hbm, right, 1),
        (slot_module_hbm, slot_module, 2),
        (counts_hbm, counts, 3),
    ):
        pltpu.make_async_copy(source, target, load_sem.at[index]).start()
    replay_load = pltpu.make_async_copy(replay_hbm, replay, load_sem.at[4])
    replay_load.start()

    barrier = pltpu.get_barrier_semaphore()

    def tell(semaphore, device):
        pl.semaphore_signal(semaphore, inc=1, device_id=device, device_id_type=MESH)

    def place(index):
        return index // halves * halves + halves - 1 - lax.rem(index, halves)

    for offset in range(1, owners):
        index = lax.rem(owner + offset, owners)

        @pl.when(place(owner) < place(index))
        def _():
            tell(barrier, {"module": index // halves, "half": lax.rem(index, halves)})

    def greet_above(index):
        @pl.when(index + 1 > z)
        def _():
            for slot in range(modules):
                tell(barrier, {"replay": index + 1, "module": slot})

    each(last, greet_above)
    def landed(ref, semaphore):
        pltpu.make_async_copy(ref, ref, semaphore).wait()

    landed(factors, load_sem.at[0])
    landed(inverses, load_sem.at[1])
    landed(slot_module, load_sem.at[2])
    landed(counts, load_sem.at[3])

    pair = 128 // tokens
    lane = lax.broadcasted_iota(jnp.int32, (share, 128), 1)
    low_lanes = lax.broadcasted_iota(jnp.int32, (examples, 2 * feat), 1) < feat

    def factored(slot):
        module = slot_module[slot]
        entries = factors[:, module].reshape(examples * tokens, width)
        doubled = jnp.concatenate([entries, entries], axis=1)
        right_high, right_low = parts_of(right[module])
        blank = jnp.zeros((feat, feat), jnp.bfloat16)
        right_rows = jnp.concatenate([right_high, blank, right_low, blank], axis=0)
        right_rows = jnp.concatenate([right_rows, right_rows], axis=1)
        v = jnp.dot(doubled, right_rows, preferred_element_type=jnp.float32)
        left_high, left_low = parts_of(left[module, pl.ds(pl.multiple_of(h * share, share), share), :])
        left_blank = jnp.zeros((share, feat), jnp.bfloat16)
        left_columns = jnp.concatenate([left_blank, left_high, left_blank, left_low], axis=1)
        u = lax.dot_general(
            left_columns, doubled, (((1,), (1,)), ((), ())), preferred_element_type=jnp.float32
        )
        return u, v

    def precondition(slot, u, v):
        v_high, v_low = parts_of(v)
        for group in range(examples // pair):
            u_pair = u[:, group * 128 : (group + 1) * 128]
            masked = []
            for inner in range(pair):
                count = counts[group * pair + inner]
                first = inner * tokens
                keep = (lane >= first) & (lane < first + count)
                masked.append(jnp.where(keep, u_pair, 0.0))
            u_high, u_low = parts_of(jnp.concatenate(masked, axis=0))
            lhs = jnp.concatenate([u_high, u_high, u_low], axis=1)
            span = slice(group * 128, (group + 1) * 128)
            rhs = jnp.concatenate([v_high[span], v_low[span], v_high[span]], axis=0)
            rows_f32[pl.ds(group * pair * share, pair * share), :] = jnp.dot(
                lhs, rhs, preferred_element_type=jnp.float32
            )
        for q in range(share // 2):
            even = rows_f32[pl.ds(2 * q, examples, stride=share), :]
            odd = rows_f32[pl.ds(2 * q + 1, examples, stride=share), :]
            outgoing[slot, :, q * 2 * feat : (q + 1) * 2 * feat] = jnp.where(low_lanes, even, odd).astype(
                jnp.bfloat16
            )

    def block_copy(slot, target_z):
        return pltpu.make_async_remote_copy(
            src_ref=outgoing.at[slot],
            dst_ref=blocks.at[block],
            send_sem=send_sem.at[0],
            recv_sem=recv_sem.at[z],
            device_id={"replay": target_z, "module": slot},
            device_id_type=MESH,
        )

    through = h == halves - 1
    skips_first = through & (z > 1)
    skips_last = through & (z < last - 1)
    hands_down = through & (z == 1) & (last > 1)
    hands_up = through & (z == last - 1) & (last > 1)

    def relay_copy(source, target_z, semaphore):
        return pltpu.make_async_remote_copy(
            src_ref=blocks.at[source],
            dst_ref=blocks.at[source],
            send_sem=semaphore,
            recv_sem=recv_sem.at[source // modules],
            device_id={"replay": target_z},
            device_id_type=MESH,
        )

    def hand_on(source_z):
        for step, semaphore, hands in ((-1, send_sem.at[2], hands_down & (source_z > z)), (1, send_sem.at[3], hands_up & (source_z < z))):

            @pl.when(hands)
            def _():
                for slot in range(modules):
                    relay_copy(source_z * modules + slot, z + step, semaphore).start()

    others = [lax.rem(x + offset, modules) for offset in range(1, modules)]

    def send_below(slot):
        def to(index):
            @pl.when((index < z) & jnp.logical_not(skips_first & (index == 0)))
            def _():
                block_copy(slot, index).start()

        each(last, to)

    def send_above(index):
        @pl.when(index + 1 > z)
        def _():
            pl.semaphore_wait(ready.at[index + 1], modules)

        @pl.when((index + 1 > z) & jnp.logical_not(skips_last & (index + 1 == last)))
        def _():
            for slot in [x, *others]:
                block_copy(slot, index + 1).start()

    order = [x, *others]
    factorings = [factored(slot) for slot in order]

    earlier = place(owner) + modules * z

    @pl.when(earlier > 0)
    def _():
        pl.semaphore_wait(barrier, earlier)

    for offset in range(1, owners):
        index = lax.rem(owner + offset, owners)

        @pl.when(place(owner) > place(index))
        def _():
            tell(ready.at[z], {"module": index // halves, "half": lax.rem(index, halves)})

    def answer_below(index):
        @pl.when(index < z)
        def _():
            for slot in range(modules):
                tell(ready.at[z], {"replay": index, "module": slot})

    each(last, answer_below)

    for index, slot in enumerate(order):
        precondition(slot, *factorings[index])
        send_below(slot)
        if index == 0:
            blocks[block] = outgoing[x]

    later = owners - 1 - place(owner)

    @pl.when(later > 0)
    def _():
        pl.semaphore_wait(ready.at[z], later)

    for slot in others:
        block_copy(slot, z).start()

    per_owner = replays // owners
    step_rows = modules * examples

    def await_plane(source_z):
        landed(blocks.at[pl.ds(source_z * modules, modules)], recv_sem.at[source_z])

    def score_copy(source, c):
        cut = pl.ds(c * chunk, chunk)
        target = source // per_owner
        return pltpu.make_async_remote_copy(
            src_ref=terms.at[pl.ds(pl.multiple_of(source * step_rows, step_rows), step_rows), cut],
            dst_ref=arrived.at[
                owner, pl.ds(pl.multiple_of((source % per_owner) * step_rows, step_rows), step_rows), cut
            ],
            send_sem=send_sem.at[1],
            recv_sem=score_recv_sem.at[c],
            device_id={"module": target // halves, "half": target % halves},
            device_id_type=MESH,
        )

    replay_load.wait()
    for first in range(0, replay.shape[1], 256):
        span = slice(first, first + 256)
        replay_t[span, :] = replay[:, span].T

    def score(planes):
        lhs = jnp.concatenate(
            [blocks[source * modules + slot] for source in planes for slot in range(modules)], axis=0
        )
        for c in range(chunks):
            cut = slice(c * chunk, (c + 1) * chunk)
            scores = jnp.dot(lhs, replay_t[:, cut], preferred_element_type=jnp.float32)
            for inner, source in enumerate(planes):
                rows = pl.ds(pl.multiple_of(source * step_rows, step_rows), step_rows)
                own = scores[inner * step_rows : (inner + 1) * step_rows]
                part[rows, cut] = own
                terms[rows, cut] = own.astype(terms.dtype)

                @pl.when(source // per_owner != owner)
                def _():
                    score_copy(source, c).start()

    each(last, send_above)
    landed(blocks.at[pl.ds(0, modules - 1)], recv_sem.at[z])
    score([z])

    def source_of(index):
        both = jnp.minimum(z, last - z)
        paired = index < 2 * both
        distance = jnp.where(paired, index // 2 + 1, index - both + 1)
        below = jnp.where(paired, 1 - index % 2, jnp.where(2 * z > last, 1, 0))
        return z + distance * (1 - 2 * below)

    def arrivals(first, count):
        planes = [source_of(first + inner) for inner in range(count)]
        for source_z in planes:
            await_plane(source_z)
            hand_on(source_z)
        score(planes)

    single = last % 2
    if single:
        arrivals(0, 1)
    each(last // 2, lambda index: arrivals(single + 2 * index, 2))

    for c in range(chunks):
        cut = slice(c * chunk, (c + 1) * chunk)
        landed(arrived.at[pl.ds(0, owners - 1), :, cut], score_recv_sem.at[c])
        first = owner * per_owner * step_rows
        summed = part[pl.ds(pl.multiple_of(first, step_rows), per_owner * step_rows), cut]
        for offset in range(1, owners):
            summed = summed + arrived[lax.rem(owner + offset, owners), :, cut].astype(jnp.float32)
        out_ref[:, cut] = summed

    skipped = jnp.where(skips_first, 1, 0) + jnp.where(skips_last, 1, 0)
    for planes in range(min(3, replays)):

        @pl.when(skipped == planes)
        def _():
            landed(blocks.at[pl.ds(0, (replays - planes) * modules - 1)], send_sem.at[0])

    for hands, semaphore in ((hands_down, send_sem.at[2]), (hands_up, send_sem.at[3])):
        if last > 1:

            @pl.when(hands)
            def _():
                landed(blocks.at[pl.ds(0, (last - 1) * modules)], semaphore)

    landed(terms.at[pl.ds(0, (replays - per_owner) * step_rows)], send_sem.at[1])


def pin(array):
    return pltpu.with_memory_space_constraint(array, pltpu.HBM)


def body(
    replays,
    modules,
    halves,
    new_factors,
    new_counts,
    new_ids,
    replay_grads,
    replay_ids,
    slot_module,
    output_inverse,
    input_inverse,
):
    examples, _, _, width = new_factors.shape
    feat = width // 2
    columns, _, depth = replay_grads.shape
    share = depth // feat
    total = replays * modules * examples
    owners = modules * halves
    rows = total // owners
    chunk = 384 if columns % 384 == 0 else columns // PIECES
    hbm = pl.BlockSpec(memory_space=pltpu.HBM)
    summed = pl.pallas_call(
        functools.partial(kernel, (replays, modules, halves, chunk)),
        out_shape=jax.ShapeDtypeStruct((rows, columns), jnp.float32),
        in_specs=[hbm] * 6,
        out_specs=pl.BlockSpec(memory_space=pltpu.VMEM),
        scratch_shapes=[
            pltpu.SMEM(slot_module.shape, jnp.int32),
            pltpu.SMEM(new_counts.shape, jnp.int32),
            pltpu.VMEM(new_factors.shape, jnp.bfloat16),
            pltpu.VMEM((columns, depth), jnp.bfloat16),
            pltpu.VMEM((depth, columns), jnp.bfloat16),
            pltpu.VMEM((2, *output_inverse.shape), jnp.float32),
            pltpu.VMEM((examples * share, 2 * feat), jnp.float32),
            pltpu.VMEM((modules, examples, depth), jnp.bfloat16),
            pltpu.VMEM((replays * modules, examples, depth), jnp.bfloat16),
            pltpu.VMEM((total, columns), jnp.float32),
            pltpu.VMEM((total, columns), TERM),
            pltpu.VMEM((owners, rows, columns), TERM),
            pltpu.SemaphoreType.DMA((5,)),
            pltpu.SemaphoreType.REGULAR((replays,)),
            pltpu.SemaphoreType.DMA((4,)),
            pltpu.SemaphoreType.DMA((replays,)),
            pltpu.SemaphoreType.DMA((columns // chunk,)),
        ],
        compiler_params=pltpu.CompilerParams(
            collective_id=0, has_side_effects=True, vmem_limit_bytes=32 * 1024 * 1024
        ),
        name="attribution",
    )(
        pin(slot_module),
        pin(new_counts),
        pin(new_factors),
        pin(replay_grads.reshape(columns, depth)),
        pin(output_inverse),
        pin(input_inverse),
    )
    self_pairs = new_ids[:, None] == replay_ids[None, :]
    return jnp.where(self_pairs, jnp.zeros((), jnp.float32), summed)


def solution(mesh):
    in_specs = (
        P(("groups", "replay", "module"), None, None, None),
        P(("groups", "replay", "module")),
        P(("groups", "module", "half")),
        P(("groups", "replay"), "module", "half"),
        P(("groups", "replay")),
        P(),
        P(),
        P(),
    )
    out_specs = P(("groups", "module", "half"), "replay")
    return jax.shard_map(
        functools.partial(body, mesh.shape["replay"], mesh.shape["module"], mesh.shape["half"]),
        mesh=mesh,
        in_specs=in_specs,
        out_specs=out_specs,
        check_vma=False,
    )
```

time: 16.3 us -> 14.8 us (0.908)
  Pallas kernels: 15.4 us -> 13.9 us
    pallas_call x1, Pallas kernels: 15.4 us -> 13.9 us  [body(): pl.pallas_call(functools.partial(kernel, (replays, modules, halves, chunk...]
where the time goes in v1:
time: 14.8 us; the launch traced here: 14.6 us
  Pallas kernels  13.9 us (94%)
  other arithmetic  0.69 us (5%)
    pallas_call x1, Pallas kernels, body(): pl.pallas_call(functools.partial(kernel, (replays, modules, halves, chunk...  13.9 us
    select_n x1, other arithmetic, body(): return jnp.where(self_pairs, jnp.zeros((), jnp.float32), summed)  0.69 us

profile of v1, /device:TPU:0, one launch (start us, length us, event | category | flops | bytes accessed | tf_op | source)
XLA Modules:
  0.0 14.6 jit_solution(13648311005874357915)
XLA Ops:
  0.0 0.0 copy-start
  0.0 0.0 copy-start.1
  0.0 13.9 %attribution.1 = f32[16,768]{1,0:T(8,128)S(1)} custom-call(s32[2]{0:T(128)} %slot_module_hbm.1, s32[8]{0:T(128)} %counts_hbm.1, bf16[8,2,64,128]{3,2,1,0:T(8,128)(2,1)} %factors_hbm.1, bf16[768,2048]{1,0:T(8,128)(2,1)} %bitcast.1, f32[2,64,64]{2,1,0:T(8,128)} %left_hbm.1, f32[2,64,64]{2,1,0:T(8,128)} %right_hbm.1), custom_call_target="tpu_custom_call" | custom-call | tf_op jit(solution)/shard_map/attribution/pallas_call | solution.py:370
  13.9 0.0 copy-done
  13.9 0.0 copy-done.1
  13.9 0.7 %compare_select_fusion = f32[16,768]{1,0:T(8,128)} fusion(f32[16,768]{1,0:T(8,128)S(1)} %attribution.1, s32[768]{0:T(1024)S(1)} %copy-done, s32[16]{0:T(128)S(1)} %copy-done.1), kind=kLoop, calls=%fused_computation | loop fusion | flops 24576 | bytes 101440 | tf_op jit(solution)/shard_map/jit(_where)/select_n | solution.py:407
Async XLA Ops:
  0.0 13.9 %copy-start = (s32[768]{0:T(1024)S(1)}, s32[768]{0:T(1024)}, u32[]{:S(2)}) copy-start(s32[768]{0:T(1024)} %param.12) | copy-start | bytes 9220
  0.0 13.9 %copy-start.1 = (s32[16]{0:T(128)S(1)}, s32[16]{0:T(128)}, u32[]{:S(2)}) copy-start(s32[16]{0:T(128)} %param.10) | copy-start | bytes 196

commit v2 on v1

--- a/solution.py
+++ b/solution.py
@@ -104,6 +104,32 @@
                 tell(barrier, {"replay": index + 1, "module": slot})
 
     each(last, greet_above)
+    def enter():
+        earlier = place(owner) + modules * z
+
+        @pl.when(earlier > 0)
+        def _():
+            pl.semaphore_wait(barrier, earlier)
+
+        for offset in range(1, owners):
+            index = lax.rem(owner + offset, owners)
+
+            @pl.when(place(owner) > place(index))
+            def _():
+                tell(ready.at[z], {"module": index // halves, "half": lax.rem(index, halves)})
+
+        def answer_below(index):
+            @pl.when(index < z)
+            def _():
+                for slot in range(modules):
+                    tell(ready.at[z], {"replay": index, "module": slot})
+
+        each(last, answer_below)
+
+    @pl.when(x > 0)
+    def _():
+        enter()
+
     def landed(ref, semaphore):
         pltpu.make_async_copy(ref, ref, semaphore).wait()
 
@@ -183,6 +209,9 @@
             device_id_type=MESH,
         )
 
+    def handed_on(source_z):
+        return (hands_down & (source_z > z)) | (hands_up & (source_z < z))
+
     def hand_on(source_z):
         for step, semaphore, hands in ((-1, send_sem.at[2], hands_down & (source_z > z)), (1, send_sem.at[3], hands_up & (source_z < z))):
 
@@ -208,47 +237,19 @@
 
         @pl.when((index + 1 > z) & jnp.logical_not(skips_last & (index + 1 == last)))
         def _():
-            for slot in [x, *others]:
+            for slot in order:
                 block_copy(slot, index + 1).start()
 
-    order = [x, *others]
+    order = [*others, x]
     factorings = [factored(slot) for slot in order]
 
-    earlier = place(owner) + modules * z
-
-    @pl.when(earlier > 0)
+    @pl.when(x == 0)
     def _():
-        pl.semaphore_wait(barrier, earlier)
-
-    for offset in range(1, owners):
-        index = lax.rem(owner + offset, owners)
-
-        @pl.when(place(owner) > place(index))
-        def _():
-            tell(ready.at[z], {"module": index // halves, "half": lax.rem(index, halves)})
-
-    def answer_below(index):
-        @pl.when(index < z)
-        def _():
-            for slot in range(modules):
-                tell(ready.at[z], {"replay": index, "module": slot})
-
-    each(last, answer_below)
+        enter()
 
     for index, slot in enumerate(order):
         precondition(slot, *factorings[index])
         send_below(slot)
-        if index == 0:
-            blocks[block] = outgoing[x]
-
-    later = owners - 1 - place(owner)
-
-    @pl.when(later > 0)
-    def _():
-        pl.semaphore_wait(ready.at[z], later)
-
-    for slot in others:
-        block_copy(slot, z).start()
 
     per_owner = replays // owners
     step_rows = modules * examples
@@ -275,6 +276,16 @@
         span = slice(first, first + 256)
         replay_t[span, :] = replay[:, span].T
 
+    blocks[block] = outgoing[x]
+    later = owners - 1 - place(owner)
+
+    @pl.when(later > 0)
+    def _():
+        pl.semaphore_wait(ready.at[z], later)
+
+    for slot in others:
+        block_copy(slot, z).start()
+
     def score(planes):
         lhs = jnp.concatenate(
             [blocks[source * modules + slot] for source in planes for slot in range(modules)], axis=0
@@ -292,10 +303,6 @@
                 def _():
                     score_copy(source, c).start()
 
-    each(last, send_above)
-    landed(blocks.at[pl.ds(0, modules - 1)], recv_sem.at[z])
-    score([z])
-
     def source_of(index):
         both = jnp.minimum(z, last - z)
         paired = index < 2 * both
@@ -303,11 +310,28 @@
         below = jnp.where(paired, 1 - index % 2, jnp.where(2 * z > last, 1, 0))
         return z + distance * (1 - 2 * below)
 
+    each(last, send_above)
+
+    def hand_over(index):
+        source_z = source_of(index)
+
+        @pl.when(handed_on(source_z))
+        def _():
+            await_plane(source_z)
+            hand_on(source_z)
+
+    each(last, hand_over)
+    landed(blocks.at[pl.ds(0, modules - 1)], recv_sem.at[z])
+    score([z])
+
     def arrivals(first, count):
         planes = [source_of(first + inner) for inner in range(count)]
         for source_z in planes:
-            await_plane(source_z)
-            hand_on(source_z)
+
+            @pl.when(jnp.logical_not(handed_on(source_z)))
+            def _():
+                await_plane(source_z)
+
         score(planes)
 
     single = last % 2

time: 14.8 us -> 13.9 us (0.939)
  Pallas kernels: 13.9 us -> 13 us
    pallas_call x1, Pallas kernels: 13.9 us -> 13 us  [body(): pl.pallas_call(functools.partial(kernel, (replays, modules, halves, chunk...]
where the time goes in v2:
time: 13.9 us; the launch traced here: 13.7 us
  Pallas kernels  13 us (94%)
  other arithmetic  0.69 us (5%)
    pallas_call x1, Pallas kernels, body(): pl.pallas_call(functools.partial(kernel, (replays, modules, halves, chunk...  13 us
    select_n x1, other arithmetic, body(): return jnp.where(self_pairs, jnp.zeros((), jnp.float32), summed)  0.69 us

profile of v2, /device:TPU:0, one launch (start us, length us, event | category | flops | bytes accessed | tf_op | source)
XLA Modules:
  0.0 13.7 jit_solution(945658413506958400)
XLA Ops:
  0.0 0.0 copy-start
  0.0 0.0 copy-start.1
  0.0 13.0 %attribution.1 = f32[16,768]{1,0:T(8,128)S(1)} custom-call(s32[2]{0:T(128)} %slot_module_hbm.1, s32[8]{0:T(128)} %counts_hbm.1, bf16[8,2,64,128]{3,2,1,0:T(8,128)(2,1)} %factors_hbm.1, bf16[768,2048]{1,0:T(8,128)(2,1)} %bitcast.1, f32[2,64,64]{2,1,0:T(8,128)} %left_hbm.1, f32[2,64,64]{2,1,0:T(8,128)} %right_hbm.1), custom_call_target="tpu_custom_call" | custom-call | tf_op jit(solution)/shard_map/attribution/pallas_call | solution.py:394
  13.0 0.0 copy-done
  13.0 0.0 copy-done.1
  13.0 0.7 %compare_select_fusion = f32[16,768]{1,0:T(8,128)} fusion(f32[16,768]{1,0:T(8,128)S(1)} %attribution.1, s32[768]{0:T(1024)S(1)} %copy-done, s32[16]{0:T(128)S(1)} %copy-done.1), kind=kLoop, calls=%fused_computation | loop fusion | flops 24576 | bytes 101440 | tf_op jit(solution)/shard_map/jit(_where)/select_n | solution.py:431
Async XLA Ops:
  0.0 13.0 %copy-start = (s32[768]{0:T(1024)S(1)}, s32[768]{0:T(1024)}, u32[]{:S(2)}) copy-start(s32[768]{0:T(1024)} %param.12) | copy-start | bytes 9220
  0.0 13.0 %copy-start.1 = (s32[16]{0:T(128)S(1)}, s32[16]{0:T(128)}, u32[]{:S(2)}) copy-start(s32[16]{0:T(128)} %param.10) | copy-start | bytes 196

commit v3 on v2

--- a/solution.py
+++ b/solution.py
@@ -87,6 +87,8 @@
     def tell(semaphore, device):
         pl.semaphore_signal(semaphore, inc=1, device_id=device, device_id_type=MESH)
 
+    others = [lax.rem(x + offset, modules) for offset in range(1, modules)]
+
     def place(index):
         return index // halves * halves + halves - 1 - lax.rem(index, halves)
 
@@ -104,8 +106,13 @@
                 tell(barrier, {"replay": index + 1, "module": slot})
 
     each(last, greet_above)
+
+    @pl.when(z > 0)
+    def _():
+        tell(barrier, {"replay": z - 1})
+
     def enter():
-        earlier = place(owner) + modules * z
+        earlier = place(owner) + modules * z + jnp.where(z < last, 1, 0)
 
         @pl.when(earlier > 0)
         def _():
@@ -121,8 +128,12 @@
         def answer_below(index):
             @pl.when(index < z)
             def _():
-                for slot in range(modules):
+                for slot in others:
                     tell(ready.at[z], {"replay": index, "module": slot})
+
+            @pl.when(index < z - 1)
+            def _():
+                tell(ready.at[z], {"replay": index})
 
         each(last, answer_below)
 
@@ -142,7 +153,7 @@
     lane = lax.broadcasted_iota(jnp.int32, (share, 128), 1)
     low_lanes = lax.broadcasted_iota(jnp.int32, (examples, 2 * feat), 1) < feat
 
-    def factored(slot):
+    def precondition(slot):
         module = slot_module[slot]
         entries = factors[:, module].reshape(examples * tokens, width)
         doubled = jnp.concatenate([entries, entries], axis=1)
@@ -157,9 +168,6 @@
         u = lax.dot_general(
             left_columns, doubled, (((1,), (1,)), ((), ())), preferred_element_type=jnp.float32
         )
-        return u, v
-
-    def precondition(slot, u, v):
         v_high, v_low = parts_of(v)
         for group in range(examples // pair):
             u_pair = u[:, group * 128 : (group + 1) * 128]
@@ -220,7 +228,6 @@
                 for slot in range(modules):
                     relay_copy(source_z * modules + slot, z + step, semaphore).start()
 
-    others = [lax.rem(x + offset, modules) for offset in range(1, modules)]
 
     def send_below(slot):
         def to(index):
@@ -231,25 +238,43 @@
         each(last, to)
 
     def send_above(index):
-        @pl.when(index + 1 > z)
-        def _():
-            pl.semaphore_wait(ready.at[index + 1], modules)
+        answers = modules - 1 + jnp.where(index > z, 1, 0)
+
+        @pl.when((index + 1 > z) & (answers > 0))
+        def _():
+            pl.semaphore_wait(ready.at[index + 1], answers)
 
         @pl.when((index + 1 > z) & jnp.logical_not(skips_last & (index + 1 == last)))
         def _():
-            for slot in order:
+            for slot in others:
                 block_copy(slot, index + 1).start()
 
+        @pl.when((index > z) & jnp.logical_not(skips_last & (index + 1 == last)))
+        def _():
+            block_copy(x, index + 1).start()
+
     order = [*others, x]
-    factorings = [factored(slot) for slot in order]
-
-    @pl.when(x == 0)
-    def _():
-        enter()
-
     for index, slot in enumerate(order):
-        precondition(slot, *factorings[index])
+        precondition(slot)
+        if index == 0:
+
+            @pl.when(x == 0)
+            def _():
+                enter()
+
         send_below(slot)
+        if index == modules - 1:
+
+            @pl.when(z < last)
+            def _():
+                block_copy(x, z + 1).start()
+
+        else:
+
+            @pl.when(slot < x)
+            def _():
+                block_copy(slot, z).start()
+
 
     per_owner = replays // owners
     step_rows = modules * examples
@@ -284,7 +309,18 @@
         pl.semaphore_wait(ready.at[z], later)
 
     for slot in others:
-        block_copy(slot, z).start()
+
+        @pl.when(slot > x)
+        def _():
+            block_copy(slot, z).start()
+
+
+    middle = replay_t.shape[0] // 2
+
+    def product(lhs, start):
+        span = slice(start, start + 128)
+        first = jnp.dot(lhs[:, :middle], replay_t[:middle, span], preferred_element_type=jnp.float32)
+        return first + jnp.dot(lhs[:, middle:], replay_t[middle:, span], preferred_element_type=jnp.float32)
 
     def score(planes):
         lhs = jnp.concatenate(
@@ -292,7 +328,7 @@
         )
         for c in range(chunks):
             cut = slice(c * chunk, (c + 1) * chunk)
-            scores = jnp.dot(lhs, replay_t[:, cut], preferred_element_type=jnp.float32)
+            scores = jnp.concatenate([product(lhs, start) for start in range(c * chunk, (c + 1) * chunk, 128)], axis=1)
             for inner, source in enumerate(planes):
                 rows = pl.ds(pl.multiple_of(source * step_rows, step_rows), step_rows)
                 own = scores[inner * step_rows : (inner + 1) * step_rows]
@@ -321,23 +357,35 @@
             hand_on(source_z)
 
     each(last, hand_over)
+
+    def await_other(source_z):
+        @pl.when(jnp.logical_not(handed_on(source_z)))
+        def _():
+            await_plane(source_z)
+
+    if last:
+        await_other(source_of(0))
     landed(blocks.at[pl.ds(0, modules - 1)], recv_sem.at[z])
-    score([z])
+    score([z, source_of(0)] if last else [z])
 
     def arrivals(first, count):
         planes = [source_of(first + inner) for inner in range(count)]
-        for source_z in planes:
-
-            @pl.when(jnp.logical_not(handed_on(source_z)))
-            def _():
-                await_plane(source_z)
-
-        score(planes)
-
-    single = last % 2
-    if single:
-        arrivals(0, 1)
-    each(last // 2, lambda index: arrivals(single + 2 * index, 2))
+
+        @pl.when(through)
+        def _():
+            for source_z in planes:
+                await_other(source_z)
+                score([source_z])
+
+        @pl.when(jnp.logical_not(through))
+        def _():
+            for source_z in planes:
+                await_other(source_z)
+            score(planes)
+
+    each((last - 1) // 2, lambda index: arrivals(1 + 2 * index, 2))
+    if last > 1 and last % 2 == 0:
+        arrivals(last - 1, 1)
 
     for c in range(chunks):
         cut = slice(c * chunk, (c + 1) * chunk)

time: 13.9 us -> 13.5 us (0.971)
  Pallas kernels: 13 us -> 12.7 us
    pallas_call x1, Pallas kernels: 13 us -> 12.7 us  [body(): pl.pallas_call(functools.partial(kernel, (replays, modules, halves, chunk...]
where the time goes in v3:
time: 13.5 us; the launch traced here: 13.4 us
  Pallas kernels  12.7 us (94%)
  other arithmetic  0.69 us (5%)
    pallas_call x1, Pallas kernels, body(): pl.pallas_call(functools.partial(kernel, (replays, modules, halves, chunk...  12.7 us
    select_n x1, other arithmetic, body(): return jnp.where(self_pairs, jnp.zeros((), jnp.float32), summed)  0.69 us

profile of v3, /device:TPU:0, one launch (start us, length us, event | category | flops | bytes accessed | tf_op | source)
XLA Modules:
  0.0 13.4 jit_solution(4840212900294584579)
XLA Ops:
  0.0 0.0 copy-start
  0.0 0.0 copy-start.1
  0.0 12.7 %attribution.1 = f32[16,768]{1,0:T(8,128)S(1)} custom-call(s32[2]{0:T(128)} %slot_module_hbm.1, s32[8]{0:T(128)} %counts_hbm.1, bf16[8,2,64,128]{3,2,1,0:T(8,128)(2,1)} %factors_hbm.1, bf16[768,2048]{1,0:T(8,128)(2,1)} %bitcast.1, f32[2,64,64]{2,1,0:T(8,128)} %left_hbm.1, f32[2,64,64]{2,1,0:T(8,128)} %right_hbm.1), custom_call_target="tpu_custom_call" | custom-call | tf_op jit(solution)/shard_map/attribution/pallas_call | solution.py:442
  12.7 0.0 copy-done
  12.7 0.0 copy-done.1
  12.7 0.7 %compare_select_fusion = f32[16,768]{1,0:T(8,128)} fusion(f32[16,768]{1,0:T(8,128)S(1)} %attribution.1, s32[768]{0:T(1024)S(1)} %copy-done, s32[16]{0:T(128)S(1)} %copy-done.1), kind=kLoop, calls=%fused_computation | loop fusion | flops 24576 | bytes 101440 | tf_op jit(solution)/shard_map/jit(_where)/select_n | solution.py:479
Async XLA Ops:
  0.0 12.7 %copy-start = (s32[768]{0:T(1024)S(1)}, s32[768]{0:T(1024)}, u32[]{:S(2)}) copy-start(s32[768]{0:T(1024)} %param.12) | copy-start | bytes 9220
  0.0 12.7 %copy-start.1 = (s32[16]{0:T(128)S(1)}, s32[16]{0:T(128)}, u32[]{:S(2)}) copy-start(s32[16]{0:T(128)} %param.10) | copy-start | bytes 196
